TPU v7x, 256 devices: a whole 4x4x8 slice. The times are simulated.
256 devices in a mesh: region: 32 (over z, x), eig: 8 (over y, core).
Axes of the slice: x: 4, y: 4, z: 8, core: 2. Of those that a mesh axis runs over, the one named last changes fastest.
Arguments:
- residual: float32 [2, 768, 32, 3072], P(None, 'region', None, 'eig'), may hold values from -6 to 6
- basis: float32 [2, 768, 64, 3072], P(None, 'region', None, 'eig'), may hold values from -0.078125 to 0.078125
- eigvecs: bfloat16 [2, 768, 64, 1024], P(None, 'region', None, 'eig'), may hold values from -0.01953125 to 0.01953125
- weights: float32 [1024], P('eig'), may hold values from 24 to 96
Outputs:
- correction: float32 [2, 768, 32, 3072], P(None, 'region', None, 'eig')
All inputs are finite; a program needn't handle non-finite values.
Results may differ from a plain program's by a relative error of at most 0.013.
Values may be sent and summed in bfloat16 or wider, within the bound.
A program may use at most 64 MiB of HBM per device.

v0:
```python
import jax
import jax.numpy as jnp
from jax import lax
from jax.sharding import PartitionSpec as P


def in_blocks(x, dim, length):
    before, after = (x.shape[:dim], x.shape[dim + 1 :])
    return jnp.moveaxis(x.reshape(*before, length, -1, *after), dim, 0)


def sum_at_owner(x, axis, dim):
    parts = in_blocks(x, dim, lax.axis_size(axis))
    arrived = lax.all_to_all(parts, axis, split_axis=0, concat_axis=0, tiled=True)
    return arrived.sum(axis=0)


def copy_for_each(x, axis):
    length = lax.axis_size(axis)
    return lax.all_to_all(jnp.broadcast_to(x[None], (length, *x.shape)), axis, 0, 0, tiled=True)


def in_order(parts, dim):
    parts = jnp.moveaxis(parts, 0, dim)
    shape = parts.shape
    return parts.reshape(*shape[:dim], shape[dim] * shape[dim + 1], *shape[dim + 2 :])


def collect(x, axis, dim):
    parts = copy_for_each(x, axis)
    return in_order(parts, dim)


def over_copies(x, axis):
    everything = copy_for_each(x, axis)
    return jnp.sum(everything, axis=0)


def sum_at_owner_2(x, axis, dim):
    length = lax.axis_size(axis)
    parts = lax.all_to_all(in_blocks(x, dim, length), axis, 0, 0, tiled=True)
    return jnp.sum(parts.astype(jnp.float32), axis=0)


def mix(form, left, right):
    return jnp.einsum(form, left, right, precision=lax.Precision.HIGHEST)


def mix_low(form, left, right):
    return jnp.einsum(form, left, right, preferred_element_type=jnp.float32)


def project(basis, residual):
    coarse_re = mix("bkc,bnc->bnk", basis[0], residual[0]) + mix(
        "bkc,bnc->bnk", basis[1], residual[1]
    )
    coarse_im = mix("bkc,bnc->bnk", basis[0], residual[1]) - mix(
        "bkc,bnc->bnk", basis[1], residual[0]
    )
    return jnp.stack([coarse_re, coarse_im], axis=1)


def contract(coarse, eig_re, eig_im):
    spec_re = mix_low("bnk,bkj->nj", coarse[:, 0], eig_re) + mix_low(
        "bnk,bkj->nj", coarse[:, 1], eig_im
    )
    spec_im = mix_low("bnk,bkj->nj", coarse[:, 1], eig_re) - mix_low(
        "bnk,bkj->nj", coarse[:, 0], eig_im
    )
    return jnp.stack([spec_re, spec_im])


def expand(weighted, eig_re, eig_im):
    lift_re = mix_low("nj,bkj->bnk", weighted[0], eig_re) - mix_low(
        "nj,bkj->bnk", weighted[1], eig_im
    )
    lift_im = mix_low("nj,bkj->bnk", weighted[0], eig_im) + mix_low(
        "nj,bkj->bnk", weighted[1], eig_re
    )
    return jnp.stack([lift_re, lift_im], axis=1)


def prolong(bas_part, lifted):
    out_re = mix("bkc,bnk->bnc", bas_part[0], lifted[:, 0]) - mix(
        "bkc,bnk->bnc", bas_part[1], lifted[:, 1]
    )
    out_im = mix("bkc,bnk->bnc", bas_part[0], lifted[:, 1]) + mix(
        "bkc,bnk->bnc", bas_part[1], lifted[:, 0]
    )
    return jnp.stack([out_re, out_im])


def shards(residual, basis, eigvecs, weights):
    partial_coarse = project(basis, residual)
    eig_re, eig_im = (eigvecs[0], eigvecs[1])
    coarse_part = sum_at_owner(partial_coarse, "eig", 0).astype(jnp.bfloat16)
    part_re = eig_re
    part_im = eig_im
    spectral = contract(collect(coarse_part, "eig", 0), part_re, part_im)
    summed = over_copies(spectral, "region")
    weighted = (summed * weights[None, None, :]).astype(jnp.bfloat16)
    part_re = eig_re
    part_im = eig_im
    lifted_part = sum_at_owner_2(expand(weighted, part_re, part_im).astype(jnp.bfloat16), "eig", 0)
    return prolong(
        basis, collect(lifted_part.astype(jnp.bfloat16), "eig", 0).astype(lifted_part.dtype)
    )


def solution(mesh):
    in_specs = (
        P(None, "region", None, "eig"),
        P(None, "region", None, "eig"),
        P(None, "region", None, "eig"),
        P("eig"),
    )
    out_specs = P(None, "region", None, "eig")
    return jax.shard_map(shards, mesh=mesh, in_specs=in_specs, out_specs=out_specs, check_vma=False)
```

profile of v0, /device:TPU:1, one launch (start us, length us, event | category | flops | bytes accessed | tf_op | source)
XLA Modules:
  0.0 112.5 jit_solution(10824305376026708309)
XLA Ops:
  0.0 4.8 %fusion.4 = f32[24,32,64]{2,1,0:T(8,128)S(1)} fusion(f32[2,24,64,384]{3,2,1,0:T(8,128)} %param.5, f32[2,24,32,384]{3,2,1,0:T(8,128)} %param.4), kind=kOutput, calls=%fused_computation.5 | convolution fusion | flops 226492416 | bytes 3735552 | tf_op jit(solution)/shard_map/bkc,bnc->bnk/dot_general | solution.py:46
  4.8 4.3 %fusion.6 = f32[24,32,64]{2,1,0:T(8,128)S(1)} fusion(f32[2,24,64,384]{3,2,1,0:T(8,128)} %param.5, f32[2,24,32,384]{3,2,1,0:T(8,128)S(1)} %copy-done.1), kind=kOutput, calls=%fused_computation.7 | convolution fusion | flops 226492416 | bytes 3735552 | tf_op jit(solution)/shard_map/bkc,bnc->bnk/dot_general | solution.py:46
  9.2 2.7 %fusion.39 = f32[24,32,64]{2,1,0:T(8,128)S(1)} fusion(f32[24,32,64]{2,1,0:T(8,128)S(1)} %fusion.4, f32[2,24,64,384]{3,2,1,0:T(8,128)S(1)} %copy-done, f32[2,24,32,384]{3,2,1,0:T(8,128)S(1)} %copy-done.1), kind=kOutput, calls=%fused_computation.32 | convolution fusion | flops 226541568 | bytes 4128768 | tf_op jit(solution)/shard_map/bkc,bnc->bnk/dot_general | solution.py:46
  11.9 2.7 %fusion.36 = f32[24,32,64]{2,1,0:T(8,128)S(1)} fusion(f32[24,32,64]{2,1,0:T(8,128)S(1)} %fusion.6, f32[2,24,64,384]{3,2,1,0:T(8,128)S(1)} %copy-done, f32[2,24,32,384]{3,2,1,0:T(8,128)S(1)} %copy-done.1), kind=kOutput, calls=%fused_computation.31 | convolution fusion | flops 226541568 | bytes 4128768 | tf_op jit(solution)/shard_map/bkc,bnc->bnk/dot_general | solution.py:46
  14.6 0.5 reshape.32
  15.1 13.8 %all_to_all.25 = f32[8,1,12288]{2,1,0:T(1,128)S(1)} all-to-all(f32[8,1,12288]{2,1,0:T(1,128)S(1)} %reshape.32), channel_id=1, replica_groups=mesh['region'=32,'eig'=8] {'eig'}, dimensions={0} | all-to-all | bytes 786432 | tf_op jit(solution)/shard_map/all_to_all | solution.py:14
  28.9 0.5 broadcast.4
  29.5 1.6 %reduce.1 = f32[8,12288]{1,0:T(8,128)S(1)} reduce(f32[8,1,12288]{2,1,0:T(1,128)S(1)} %all_to_all.25, f32[]{:T(128)} %broadcast.4), dimensions={1}, to_apply=%all_to_all.15.reduce_sub_computation | reduce | bytes 786436 | tf_op jit(solution)/shard_map/all_to_all | solution.py:14
  31.0 0.3 reshape.33
  31.5 0.3 reshape.34
  31.8 9.1 %all_to_all.26 = bf16[8,2,6144]{2,1,0:T(2,128)(2,1)S(1)} all-to-all(bf16[8,2,6144]{2,1,0:T(2,128)(2,1)S(1)} %reshape.34), channel_id=1, replica_groups=mesh['region'=32,'eig'=8] {'eig'}, dimensions={0} | all-to-all | bytes 393216 | tf_op jit(solution)/shard_map/all_to_all | solution.py:20
  42.4 36.9 %all_to_all.27 = f32[32,2,32,128]{3,2,1,0:T(8,128)S(1)} all-to-all(f32[32,2,32,128]{3,2,1,0:T(8,128)S(1)} %broadcast_in_dim.7), channel_id=1, replica_groups=mesh['region'=32,'eig'=8] {'region'}, dimensions={0} | all-to-all | bytes 2097152 | tf_op jit(solution)/shard_map/all_to_all | solution.py:20
  79.4 0.5 fusion.56
  79.8 0.5 fusion.62
  80.3 0.5 fusion.47
  80.8 0.5 fusion.46
  81.7 11.2 %all_to_all.28 = bf16[8,2,6144]{2,1,0:T(2,128)(2,1)S(1)} all-to-all(bf16[8,2,6144]{2,1,0:T(2,128)(2,1)S(1)} %reshape.36), channel_id=1, replica_groups=mesh['region'=32,'eig'=8] {'eig'}, dimensions={0} | all-to-all | bytes 393216 | tf_op jit(solution)/shard_map/all_to_all | solution.py:41
  93.3 0.3 reshape.38
  93.6 9.2 %all_to_all.29 = bf16[8,2,6144]{2,1,0:T(2,128)(2,1)S(1)} all-to-all(bf16[8,2,6144]{2,1,0:T(2,128)(2,1)S(1)} %reshape.38), channel_id=1, replica_groups=mesh['region'=32,'eig'=8] {'eig'}, dimensions={0} | all-to-all | bytes 393216 | tf_op jit(solution)/shard_map/all_to_all | solution.py:20
  103.2 2.8 %fusion = f32[24,32,384]{2,1,0:T(8,128)S(1)} fusion(f32[2,24,64,384]{3,2,1,0:T(8,128)} %param.5, bf16[24,2,32,64]{3,2,0,1:T(8,128)(2,1)S(1)} %bitcast.142), kind=kOutput, calls=%fused_computation.1 | convolution fusion | flops 226492416 | bytes 3735552 | tf_op jit(solution)/shard_map/bkc,bnk->bnc/dot_general | solution.py:46
  106.0 2.7 %fusion.2 = f32[24,32,384]{2,1,0:T(8,128)S(1)} fusion(f32[2,24,64,384]{3,2,1,0:T(8,128)} %param.5, bf16[24,2,32,64]{3,2,0,1:T(8,128)(2,1)S(1)} %bitcast.143), kind=kOutput, calls=%fused_computation.3 | convolution fusion | flops 226492416 | bytes 3735552 | tf_op jit(solution)/shard_map/bkc,bnk->bnc/dot_general | solution.py:46
  108.7 1.1 fusion.33
  109.8 1.1 fusion.27
  110.9 1.6 %pad_maximum_fusion = f32[2,24,32,384]{3,2,1,0:T(8,128)} fusion(f32[1,24,32,384]{3,2,1,0:T(8,128)S(1)} %fusion.33, f32[1,24,32,384]{3,2,1,0:T(8,128)S(1)} %fusion.27), kind=kLoop, calls=%fused_computation | loop fusion | flops 589824 | bytes 4718592 | tf_op jit(solution)/shard_map/stack | solution.py:90
  (33 shorter events, 2.8 us)
Async XLA Ops:
  0.0 4.8 %copy-start.1 = (f32[2,24,32,384]{3,2,1,0:T(8,128)S(1)}, f32[2,24,32,384]{3,2,1,0:T(8,128)}, u32[]{:S(2)}) copy-start(f32[2,24,32,384]{3,2,1,0:T(8,128)} %param.4) | copy-start | bytes 7077892
  0.0 9.1 %copy-start = (f32[2,24,64,384]{3,2,1,0:T(8,128)S(1)}, f32[2,24,64,384]{3,2,1,0:T(8,128)}, u32[]{:S(2)}) copy-start(f32[2,24,64,384]{3,2,1,0:T(8,128)} %param.5) | copy-start | bytes 14155780
  31.0 10.2 %copy-start.2 = (bf16[2,24,64,128]{3,2,1,0:T(8,128)(2,1)S(1)}, bf16[2,24,64,128]{3,2,1,0:T(8,128)(2,1)}, u32[]{:S(2)}) copy-start(bf16[2,24,64,128]{3,2,1,0:T(8,128)(2,1)} %param.6) | copy-start | bytes 2359300
  42.0 37.4 %copy-start.3 = (f32[128]{0:T(128)S(1)}, f32[128]{0:T(128)}, u32[]{:S(2)}) copy-start(f32[128]{0:T(128)} %param.7) | copy-start | bytes 1540
  80.3 28.4 %slice-start = ((s8[4718592]{0:T(1024)(128)(4,1)}), s8[524288]{0:T(1024)(128)(4,1)S(1)}, s32[]{:S(2)}) async-start(s8[4718592]{0:T(1024)(128)(4,1)} %bitcast.140), calls=%async_computation.5 | async-start | bytes 1048576
  103.1 5.6 %slice-start.1 = ((s8[4718592]{0:T(1024)(128)(4,1)}), s8[4194304]{0:T(1024)(128)(4,1)S(1)}, s32[]{:S(2)}) async-start(s8[4718592]{0:T(1024)(128)(4,1)} %bitcast.140), calls=%async_computation.6 | async-start | bytes 8388608
where the time goes:
time: 113 us
  blocking collectives  80.2 us (71%)
  matrix products  25.1 us (22%)
  other arithmetic  3.53 us (3%)
  local copies, waits for them, and re-layouts  3.41 us (3%)
    all_to_all x3, blocking collectives, copy_for_each(): lax.all_to_all(jnp.broadcast_to(x[None], (length, *x.shape)), axis, 0, 0,...  55.2 us
    dot_general x8, matrix products, mix(): return jnp.einsum(form, left, right, precision=lax.Precision.HIGHEST)  22.3 us
    all_to_all x1, blocking collectives, sum_at_owner(): lax.all_to_all(parts, axis, split_axis=0, concat_axis=0, tiled=True)  13.8 us
    all_to_all x1, blocking collectives, sum_at_owner_2(): parts = lax.all_to_all(in_blocks(x, dim, length), axis, 0, 0, tiled=True)  11.2 us
    dot_general x8, matrix products, mix_low(): return jnp.einsum(form, left, right, preferred_element_type=jnp.float32)  2.81 us
    unnamed x22, local copies, waits for them, and re-layouts  2.72 us

commit v1 on v0

v1 whole, which is shorter than its diff:
```python
import functools

import jax
import jax.numpy as jnp
from jax import lax
from jax.experimental import pallas as pl
from jax.experimental.pallas import tpu as pltpu
from jax.sharding import PartitionSpec as P

MESH = pl.DeviceIdType.MESH
BF16 = jnp.bfloat16
F32 = jnp.float32

BLOCKS = 24
COLS = 32
BASIS = 64
COMP = 384
EIGV = 128
SHARE = 8
CHUNKS = BLOCKS // SHARE
X, Y, Z = 4, 4, 8
GROUP = 4
FAR_FIRST = ((2, 0), (2, 1), (1, 0), (1, 1), (3, 0), (3, 1), (0, 1))
Z_FAR_FIRST = (4, 3, 5, 2, 6, 1, 7)
X_FAR_FIRST = (2, 1, 3)


def signs(rows):
    lane = lax.broadcasted_iota(jnp.int32, (rows, 2 * BASIS), 1)
    return jnp.where(lane < BASIS, 1.0, -1.0).astype(F32)


def coefficients(
    res,
    bas,
    eig,
    wts,
    bas_out,
    lift_out,
    rv,
    bv,
    ev,
    wv,
    part,
    part_in,
    coarse,
    lpart,
    lpart_in,
    lift,
    spec,
    spec_in,
    zown,
    zin,
    wall,
    load_sem,
    eig_sem,
    rs_send,
    rs_recv,
    ag_send,
    ag_recv,
    x_send,
    x_recv,
    z_send,
    z_recv,
    w_send,
    w_recv,
):
    region = lax.axis_index("region")
    me = lax.axis_index("eig")
    x, z = lax.rem(region, X), lax.div(region, X)
    core, y = lax.rem(me, 2), lax.div(me, 2)

    loads = []
    for g in range(BLOCKS // GROUP):
        span = pl.ds(g * GROUP, GROUP)
        pair = (
            pltpu.make_async_copy(bas.at[:, span], bv.at[:, span], load_sem.at[0, g]),
            pltpu.make_async_copy(res.at[:, span], rv.at[:, span], load_sem.at[1, g]),
        )
        for copy in pair:
            copy.start()
        loads.append(pair)
    eig_load = pltpu.make_async_copy(eig, ev, eig_sem)
    eig_load.start()

    def eig_peer(dy, dc):
        return (region, lax.rem(y + dy, Y) * 2 + lax.rem(core + dc, 2))

    def x_peer(dx):
        return (z * X + lax.rem(x + dx, X), me)

    def z_peer(dz):
        return (lax.rem(z + dz, Z) * X + x, me)

    peers = [eig_peer(*d) for d in FAR_FIRST]
    peers += [x_peer(d) for d in X_FAR_FIRST] + [z_peer(d) for d in Z_FAR_FIRST]
    barrier = pltpu.get_barrier_semaphore()
    for peer in peers:
        pl.semaphore_signal(barrier, inc=1, device_id=peer, device_id_type=MESH)

    sent = []

    def send(src, dst, send_sem, recv_sem, peer):
        copy = pltpu.make_async_remote_copy(
            src_ref=src,
            dst_ref=dst,
            send_sem=send_sem,
            recv_sem=recv_sem,
            device_id=peer,
            device_id_type=MESH,
        )
        copy.start()
        sent.append(copy)
        return copy

    def scatter(which, c, own, inbox):
        copies = []
        for i, d in enumerate(FAR_FIRST):
            peer = eig_peer(*d)
            copies.append(
                send(
                    own.at[SHARE * c + peer[1]],
                    inbox.at[c, i],
                    rs_send.at[which, c, i],
                    rs_recv.at[which, c, i],
                    peer,
                )
            )
        return copies

    def gather(which, c, copies, own, inbox, whole):
        mine = SHARE * c + me
        total = own[mine].astype(F32)
        for i in reversed(range(len(FAR_FIRST))):
            copies[i].wait_recv()
            total += inbox[c, i].astype(F32)
        whole[mine] = total.astype(BF16)
        out = []
        for i, d in enumerate(FAR_FIRST):
            out.append(
                send(
                    whole.at[mine],
                    whole.at[mine],
                    ag_send.at[which, c, i],
                    ag_recv.at[which, c, i],
                    eig_peer(*d),
                )
            )
        return out

    sign = signs(COLS)

    def project(b):
        r = jnp.concatenate([rv[0, b], rv[1, b]], 0).astype(BF16)
        k = jnp.concatenate([bv[0, b], bv[1, b]], 0).astype(BF16)
        bas_out[b] = k
        p = lax.dot_general(r, k, (((1,), (1,)), ((), ())), preferred_element_type=F32)
        part[b] = (p[:COLS] * sign + pltpu.roll(p[COLS:], BASIS, 1)).astype(BF16)

    rs = []
    for c in range(CHUNKS):
        for g in range(c * SHARE // GROUP, (c + 1) * SHARE // GROUP):
            for copy in loads[g]:
                copy.wait()
            for b in range(g * GROUP, (g + 1) * GROUP):
                project(b)
        if c == 0:
            pl.semaphore_wait(barrier, len(peers))
        rs.append(scatter(0, c, part, part_in))

    eig_load.wait()
    for b in range(BLOCKS):
        re, im = ev[0, b], ev[1, b]
        wv[b, :BASIS, :EIGV] = re
        wv[b, :BASIS, EIGV:] = -im
        wv[b, BASIS:, :EIGV] = im
        wv[b, BASIS:, EIGV:] = re

    ag = [gather(0, c, rs[c], part, part_in, coarse) for c in range(CHUNKS)]
    total = jnp.zeros((COLS, 2 * EIGV), F32)
    for c in range(CHUNKS):
        for copy in ag[c]:
            copy.wait_recv()
        for b in range(SHARE * c, SHARE * (c + 1)):
            total += jnp.dot(coarse[b], wv[b], preferred_element_type=F32)

    half = COLS // 2
    for q in range(X):
        row, col = half * (q // 2), EIGV * (q % 2)
        spec[q] = total[row : row + half, col : col + EIGV].astype(BF16)
    xs = [
        send(spec.at[x_peer(d)[0] - z * X], spec_in.at[i], x_send.at[i], x_recv.at[i], x_peer(d))
        for i, d in enumerate(X_FAR_FIRST)
    ]
    quarter = spec[x].astype(F32)
    for i in reversed(range(len(xs))):
        xs[i].wait_recv()
        quarter += spec_in[i].astype(F32)
    zown[...] = quarter.astype(BF16)
    zs = [
        send(zown, zin.at[i], z_send.at[i], z_recv.at[i], z_peer(d))
        for i, d in enumerate(Z_FAR_FIRST)
    ]
    for i in reversed(range(len(zs))):
        zs[i].wait_recv()
        quarter += zin[i].astype(F32)
    wall[x] = (quarter * wts[...]).astype(BF16)
    ws = [
        send(wall.at[x], wall.at[x], w_send.at[i], w_recv.at[i], x_peer(d))
        for i, d in enumerate(X_FAR_FIRST)
    ]
    for copy in ws:
        copy.wait_recv()
    weighted = jnp.concatenate(
        [
            jnp.concatenate([wall[0], wall[1]], 1),
            jnp.concatenate([wall[2], wall[3]], 1),
        ],
        0,
    )

    rs = []
    for c in range(CHUNKS):
        for b in range(SHARE * c, SHARE * (c + 1)):
            lpart[b] = lax.dot_general(
                weighted, wv[b], (((1,), (1,)), ((), ())), preferred_element_type=F32
            ).astype(BF16)
        rs.append(scatter(1, c, lpart, lpart_in))
    ag = [gather(1, c, rs[c], lpart, lpart_in, lift) for c in range(CHUNKS)]
    for c in range(CHUNKS):
        for copy in ag[c]:
            copy.wait_recv()
        for b in range(SHARE * c, SHARE * (c + 1)):
            lift_out[b] = lift[b]
    for copy in sent:
        copy.wait_send()


def prolong(lift, bas, out):
    sign = signs(COLS)
    for b in range(lift.shape[0]):
        l = lift[b].astype(F32)
        rows = jnp.concatenate([l * sign, pltpu.roll(l, BASIS, 1)], 0).astype(BF16)
        both = jnp.dot(rows, bas[b], preferred_element_type=F32)
        out[0, b] = both[:COLS]
        out[1, b] = both[COLS:]


def shards(residual, basis, eigvecs, weights):
    any_spec = pl.BlockSpec(memory_space=pl.ANY)
    vmem_spec = pl.BlockSpec(memory_space=pltpu.VMEM)
    sem = pltpu.SemaphoreType.DMA
    n = len(FAR_FIRST)
    block = (COLS, 2 * BASIS)
    bas, lift = pl.pallas_call(
        coefficients,
        out_shape=(
            jax.ShapeDtypeStruct((BLOCKS, 2 * BASIS, COMP), BF16),
            jax.ShapeDtypeStruct((BLOCKS, *block), BF16),
        ),
        in_specs=[any_spec, any_spec, any_spec, vmem_spec],
        out_specs=(vmem_spec, vmem_spec),
        scratch_shapes=[
            pltpu.VMEM((2, BLOCKS, COLS, COMP), F32),
            pltpu.VMEM((2, BLOCKS, BASIS, COMP), F32),
            pltpu.VMEM((2, BLOCKS, BASIS, EIGV), BF16),
            pltpu.VMEM((BLOCKS, 2 * BASIS, 2 * EIGV), BF16),
            pltpu.VMEM((BLOCKS, *block), BF16),
            pltpu.VMEM((CHUNKS, n, *block), BF16),
            pltpu.VMEM((BLOCKS, *block), BF16),
            pltpu.VMEM((BLOCKS, *block), BF16),
            pltpu.VMEM((CHUNKS, n, *block), BF16),
            pltpu.VMEM((BLOCKS, *block), BF16),
            pltpu.VMEM((X, COLS // 2, EIGV), BF16),
            pltpu.VMEM((X - 1, COLS // 2, EIGV), BF16),
            pltpu.VMEM((COLS // 2, EIGV), BF16),
            pltpu.VMEM((Z - 1, COLS // 2, EIGV), BF16),
            pltpu.VMEM((X, COLS // 2, EIGV), BF16),
            sem((2, BLOCKS // GROUP)),
            sem,
            sem((2, CHUNKS, n)),
            sem((2, CHUNKS, n)),
            sem((2, CHUNKS, n)),
            sem((2, CHUNKS, n)),
            sem((X - 1,)),
            sem((X - 1,)),
            sem((Z - 1,)),
            sem((Z - 1,)),
            sem((X - 1,)),
            sem((X - 1,)),
        ],
        compiler_params=pltpu.CompilerParams(
            collective_id=0, has_side_effects=True, vmem_limit_bytes=24 << 20
        ),
    )(residual, basis, eigvecs, weights.reshape(1, EIGV))

    step = 4
    return pl.pallas_call(
        prolong,
        grid=(BLOCKS // step,),
        out_shape=jax.ShapeDtypeStruct((2, BLOCKS, COLS, COMP), F32),
        in_specs=[
            pl.BlockSpec((step, *block), lambda i: (i, 0, 0)),
            pl.BlockSpec((step, 2 * BASIS, COMP), lambda i: (i, 0, 0)),
        ],
        out_specs=pl.BlockSpec((2, step, COLS, COMP), lambda i: (0, i, 0, 0)),
        compiler_params=pltpu.CompilerParams(vmem_limit_bytes=16 << 20),
    )(lift, bas)


def solution(mesh):
    in_specs = (
        P(None, "region", None, "eig"),
        P(None, "region", None, "eig"),
        P(None, "region", None, "eig"),
        P("eig"),
    )
    out_specs = P(None, "region", None, "eig")
    return jax.shard_map(shards, mesh=mesh, in_specs=in_specs, out_specs=out_specs, check_vma=False)
```

time: 113 us -> 50.1 us (0.44)
  blocking collectives: 80.2 us -> 0 us
  Pallas kernels: 0 us -> 44.1 us
  matrix products: 25.1 us -> 0 us
  other arithmetic: 3.53 us -> 0 us
  local copies, waits for them, and re-layouts: 3.41 us -> 5.79 us
    all_to_all x5 -> x0, blocking collectives: 80.2 us -> none  [the longest x3 55.2 us: copy_for_each(): lax.all_to_all(jnp.broadcast_to(x[None], (length, *x.shape)), axis, 0, 0,...]
    pallas_call x0 -> x2, Pallas kernels: none -> 44.1 us  [the longest x1 40.8 us: shards(): pl.pallas_call(coefficients, out_shape=(jax.ShapeDtypeStruct((BLOCKS, 2 *...]
    dot_general x16 -> x0, matrix products: 25.1 us -> none  [the longest x8 22.3 us: mix(): return jnp.einsum(form, left, right, precision=lax.Precision.HIGHEST)]
    unnamed x22 -> x8, local copies, waits for them, and re-layouts: 2.72 us -> 5.79 us
    all_to_all x1 -> x0, other arithmetic: 1.57 us -> none  [sum_at_owner(): lax.all_to_all(parts, axis, split_axis=0, concat_axis=0, tiled=True)]
    another operation x2 -> x0, other arithmetic: 1.56 us -> none  [the longest x1 1.56 us: prolong(): return jnp.stack([out_re, out_im])]
where the time goes in v1:
time: 50.1 us; the launch traced here: 49.9 us
  Pallas kernels  44.1 us (88%)
  local copies, waits for them, and re-layouts  5.79 us (12%)
    pallas_call x1, Pallas kernels, shards(): pl.pallas_call(coefficients, out_shape=(jax.ShapeDtypeStruct((BLOCKS, 2 *...  40.8 us
    unnamed x8, local copies, waits for them, and re-layouts  5.79 us
    pallas_call x1, Pallas kernels, shards(): pl.pallas_call(prolong, grid=(BLOCKS // step,), out_shape=jax.ShapeDtypeS...  3.33 us

profile of v1, /device:TPU:1, one launch (start us, length us, event | category | flops | bytes accessed | tf_op | source)
XLA Modules:
  0.0 49.9 jit_solution(5333056913025961677)
XLA Ops:
  0.0 0.0 copy-start
  0.0 2.3 %copy-done = f32[2,24,64,384]{3,2,1,0:T(8,128)S(1)} copy-done((f32[2,24,64,384]{3,2,1,0:T(8,128)S(1)}, f32[2,24,64,384]{3,2,1,0:T(8,128)}, u32[]{:S(2)}) %copy-start) | copy-done | bytes 4718616
  2.3 0.0 copy-start.1
  2.3 1.7 %copy-done.1 = f32[2,24,32,384]{3,2,1,0:T(8,128)S(1)} copy-done((f32[2,24,32,384]{3,2,1,0:T(8,128)S(1)}, f32[2,24,32,384]{3,2,1,0:T(8,128)}, u32[]{:S(2)}) %copy-start.1) | copy-done | bytes 2359320
  4.0 0.0 copy-start.2
  4.0 1.1 %copy-done.2 = bf16[2,24,64,128]{3,2,1,0:T(8,128)(2,1)S(1)} copy-done((bf16[2,24,64,128]{3,2,1,0:T(8,128)(2,1)S(1)}, bf16[2,24,64,128]{3,2,1,0:T(8,128)(2,1)}, u32[]{:S(2)}) %copy-start.2) | copy-done | bytes 786456
  5.1 0.0 copy-start.3
  5.1 0.7 %copy-done.3 = f32[128]{0:T(128)S(1)} copy-done((f32[128]{0:T(128)S(1)}, f32[128]{0:T(128)}, u32[]{:S(2)}) %copy-start.3) | copy-done | bytes 536
  5.8 40.8 %shard_map.46 = (bf16[24,128,384]{2,1,0:T(8,128)(2,1)S(1)}, bf16[24,32,128]{2,1,0:T(8,128)(2,1)S(1)}) custom-call(f32[2,24,32,384]{3,2,1,0:T(8,128)S(1)} %copy-done.1, f32[2,24,64,384]{3,2,1,0:T(8,128)S(1)} %copy-done, bf16[2,24,64,128]{3,2,1,0:T(8,128)(2,1)S(1)} %copy-done.2, f32[1,128]{1,0:T(1,128)S(1)} %bitcast.1), custom_call_target="tpu_custom_call" | custom-call | tf_op jit(solution)/shard_map/pallas_call | solution.py:255
  46.6 3.3 %shard_map.47 = f32[2,24,32,384]{3,2,1,0:T(8,128)} custom-call(bf16[24,32,128]{2,1,0:T(8,128)(2,1)S(1)} %get-tuple-element.7.lift, bf16[24,128,384]{2,1,0:T(8,128)(2,1)S(1)} %get-tuple-element.8.bas), custom_call_target="tpu_custom_call" | custom-call | tf_op jit(solution)/shard_map/pallas_call | solution.py:298
Async XLA Ops:
  0.0 2.3 %copy-start = (f32[2,24,64,384]{3,2,1,0:T(8,128)S(1)}, f32[2,24,64,384]{3,2,1,0:T(8,128)}, u32[]{:S(2)}) copy-start(f32[2,24,64,384]{3,2,1,0:T(8,128)} %bas.1) | copy-start | bytes 14155780
  2.3 1.7 %copy-start.1 = (f32[2,24,32,384]{3,2,1,0:T(8,128)S(1)}, f32[2,24,32,384]{3,2,1,0:T(8,128)}, u32[]{:S(2)}) copy-start(f32[2,24,32,384]{3,2,1,0:T(8,128)} %res.1) | copy-start | bytes 7077892
  4.0 1.1 %copy-start.2 = (bf16[2,24,64,128]{3,2,1,0:T(8,128)(2,1)S(1)}, bf16[2,24,64,128]{3,2,1,0:T(8,128)(2,1)}, u32[]{:S(2)}) copy-start(bf16[2,24,64,128]{3,2,1,0:T(8,128)(2,1)} %eig.1) | copy-start | bytes 2359300
  5.1 0.7 %copy-start.3 = (f32[128]{0:T(128)S(1)}, f32[128]{0:T(128)}, u32[]{:S(2)}) copy-start(f32[128]{0:T(128)} %param.7) | copy-start | bytes 1540

commit v2 on v1

v2 whole, which is shorter than its diff:
```python
import functools

import jax
import jax.numpy as jnp
from jax import lax
from jax.experimental import pallas as pl
from jax.experimental.pallas import tpu as pltpu
from jax.sharding import PartitionSpec as P

MESH = pl.DeviceIdType.MESH
BF16 = jnp.bfloat16
F32 = jnp.float32

BLOCKS = 24
COLS = 32
BASIS = 64
COMP = 384
EIGV = 128
X, Y, Z = 4, 4, 8
CHUNK = 8
HALF = CHUNK // 2
CHUNKS = BLOCKS // CHUNK
GROUP = 4
ALONG_X = (2, 1, 3)
ALONG_Y = (2, 1, 3)
ALONG_Z = (4, 3, 5, 2, 6, 1, 7)


def signs(rows):
    lane = lax.broadcasted_iota(jnp.int32, (rows, 2 * BASIS), 1)
    return jnp.where(lane < BASIS, 1.0, -1.0).astype(F32)


def coefficients(
    res,
    bas,
    eig,
    wts,
    bas_out,
    lift_out,
    rv,
    bv,
    ev,
    wtv,
    wv,
    part,
    core_in,
    chip,
    chip_in,
    whole,
    spec,
    spec_in,
    zown,
    zin,
    load_sem,
    eig_sem,
    c_send,
    c_recv,
    y_send,
    y_recv,
    g_send,
    g_recv,
    x_send,
    x_recv,
    z_send,
    z_recv,
):
    region = lax.axis_index("region")
    me = lax.axis_index("eig")
    x, z = lax.rem(region, X), lax.div(region, X)
    core, y = lax.rem(me, 2), lax.div(me, 2)

    loads = []
    for g in range(BLOCKS // GROUP):
        span = pl.ds(g * GROUP, GROUP)
        pair = (
            pltpu.make_async_copy(bas.at[:, span], bv.at[:, span], load_sem.at[0, g]),
            pltpu.make_async_copy(res.at[:, span], rv.at[:, span], load_sem.at[1, g]),
        )
        for copy in pair:
            copy.start()
        loads.append(pair)
    eig_load = pltpu.make_async_copy(eig, ev, eig_sem.at[0])
    wts_load = pltpu.make_async_copy(wts, wtv, eig_sem.at[1])
    eig_load.start()
    wts_load.start()

    partner = (region, y * 2 + 1 - core)
    x_peers = [(z * X + lax.rem(x + d, X), me) for d in ALONG_X]
    y_peers = [(region, lax.rem(y + d, Y) * 2 + core) for d in ALONG_Y]
    z_peers = [(lax.rem(z + d, Z) * X + x, me) for d in ALONG_Z]
    peers = [partner] + x_peers + y_peers + z_peers
    barrier = pltpu.get_barrier_semaphore()
    for peer in peers:
        pl.semaphore_signal(barrier, inc=1, device_id=peer, device_id_type=MESH)

    sent = []

    def send(src, dst, send_sem, recv_sem, peer):
        copy = pltpu.make_async_remote_copy(
            src_ref=src,
            dst_ref=dst,
            send_sem=send_sem,
            recv_sem=recv_sem,
            device_id=peer,
            device_id_type=MESH,
        )
        copy.start()
        sent.append(copy)
        return copy

    def mine(c):
        return pl.ds(CHUNK * c + HALF * core, HALF)

    def to_partner(w, c):
        theirs = pl.ds(CHUNK * c + HALF * (1 - core), HALF)
        return send(
            part.at[w, theirs], core_in.at[w, c], c_send.at[w, c], c_recv.at[w, c], partner
        )

    def along_y(w, c, copy):
        copy.wait_recv()
        total = part[w, mine(c)].astype(F32) + core_in[w, c].astype(F32)
        chip[w, c] = total.astype(BF16)
        return [
            send(chip.at[w, c], chip_in.at[w, c, i], y_send.at[w, c, i], y_recv.at[w, c, i], peer)
            for i, peer in enumerate(y_peers)
        ]

    def to_chip(w, c, copies):
        total = chip[w, c].astype(F32)
        for i in (1, 2, 0):
            copies[i].wait_recv()
            total += chip_in[w, c, i].astype(F32)
        whole[w, mine(c)] = total.astype(BF16)
        done = whole.at[w, mine(c)]
        return send(done, done, g_send.at[w, c], g_recv.at[w, c], partner)

    def exchange(w, produce, between, consume):
        pair, over_y, over_chip = {}, {}, {}
        for c in range(CHUNKS):
            produce(c)
            if w == 0 and c == 0:
                pl.semaphore_wait(barrier, len(peers))
            pair[c] = to_partner(w, c)
            if c > 0:
                over_y[c - 1] = along_y(w, c - 1, pair[c - 1])
        between()
        over_y[CHUNKS - 1] = along_y(w, CHUNKS - 1, pair[CHUNKS - 1])
        for c in range(CHUNKS):
            over_chip[c] = to_chip(w, c, over_y[c])
            if c > 0:
                over_chip[c - 1].wait_recv()
                consume(c - 1)
        over_chip[CHUNKS - 1].wait_recv()
        consume(CHUNKS - 1)

    def blocks_of(c):
        return range(CHUNK * c, CHUNK * (c + 1))

    sign = signs(COLS)

    def project(c):
        for g in range(c * CHUNK // GROUP, (c + 1) * CHUNK // GROUP):
            for copy in loads[g]:
                copy.wait()
            for b in range(g * GROUP, (g + 1) * GROUP):
                r = jnp.concatenate([rv[0, b], rv[1, b]], 0).astype(BF16)
                k = jnp.concatenate([bv[0, b], bv[1, b]], 0).astype(BF16)
                bas_out[b] = k
                p = lax.dot_general(r, k, (((1,), (1,)), ((), ())), preferred_element_type=F32)
                part[0, b] = (p[:COLS] * sign + pltpu.roll(p[COLS:], BASIS, 1)).astype(BF16)

    def pack():
        eig_load.wait()
        wts_load.wait()
        for b in range(BLOCKS):
            re, im = ev[0, b], ev[1, b]
            wv[b, :BASIS, :EIGV] = re
            wv[b, :BASIS, EIGV:] = -im
            wv[b, BASIS:, :EIGV] = im
            wv[b, BASIS:, EIGV:] = re

    sums = []

    def contract(c):
        total = sums.pop() if sums else jnp.zeros((COLS, 2 * EIGV), F32)
        for b in blocks_of(c):
            total += jnp.dot(whole[0, b], wv[b], preferred_element_type=F32)
        sums.append(total)

    exchange(0, project, pack, contract)

    total = sums.pop()
    spec[...] = total.astype(BF16)
    xs = [
        send(spec, spec_in.at[i], x_send.at[i], x_recv.at[i], peer)
        for i, peer in enumerate(x_peers)
    ]
    for i in reversed(range(len(xs))):
        xs[i].wait_recv()
        total += spec_in[i].astype(F32)
    zown[...] = total.astype(BF16)
    zs = [
        send(zown, zin.at[i], z_send.at[i], z_recv.at[i], peer) for i, peer in enumerate(z_peers)
    ]
    for i in reversed(range(len(zs))):
        zs[i].wait_recv()
        total += zin[i].astype(F32)
    weighted = (total * jnp.concatenate([wtv[...], wtv[...]], 1)).astype(BF16)

    def expand(c):
        for b in blocks_of(c):
            part[1, b] = lax.dot_general(
                weighted, wv[b], (((1,), (1,)), ((), ())), preferred_element_type=F32
            ).astype(BF16)

    def hand_on(c):
        for b in blocks_of(c):
            lift_out[b] = whole[1, b]

    exchange(1, expand, lambda: None, hand_on)
    for copy in sent:
        copy.wait_send()


def prolong(lift, bas, out, ov, sem):
    sign = signs(COLS)
    copies = []
    for c in range(CHUNKS):
        for b in range(CHUNK * c, CHUNK * (c + 1)):
            l = lift[b].astype(F32)
            rows = jnp.concatenate([l * sign, pltpu.roll(l, BASIS, 1)], 0).astype(BF16)
            both = jnp.dot(rows, bas[b], preferred_element_type=F32)
            ov[0, b] = both[:COLS]
            ov[1, b] = both[COLS:]
        span = pl.ds(CHUNK * c, CHUNK)
        copies.append(pltpu.make_async_copy(ov.at[:, span], out.at[:, span], sem.at[c]))
        copies[-1].start()
    for copy in copies:
        copy.wait()


def shards(residual, basis, eigvecs, weights):
    hbm_spec = pl.BlockSpec(memory_space=pltpu.HBM)
    vmem_spec = pl.BlockSpec(memory_space=pltpu.VMEM)
    sem = pltpu.SemaphoreType.DMA
    block = (COLS, 2 * BASIS)
    spectral = (COLS, 2 * EIGV)
    args = [
        pltpu.with_memory_space_constraint(a, pltpu.HBM)
        for a in (residual, basis, eigvecs, weights.reshape(1, EIGV))
    ]
    bas, lift = pl.pallas_call(
        coefficients,
        out_shape=(
            jax.ShapeDtypeStruct((BLOCKS, 2 * BASIS, COMP), BF16),
            jax.ShapeDtypeStruct((BLOCKS, *block), BF16),
        ),
        in_specs=[hbm_spec] * 4,
        out_specs=(vmem_spec, vmem_spec),
        scratch_shapes=[
            pltpu.VMEM((2, BLOCKS, COLS, COMP), F32),
            pltpu.VMEM((2, BLOCKS, BASIS, COMP), F32),
            pltpu.VMEM((2, BLOCKS, BASIS, EIGV), BF16),
            pltpu.VMEM((1, EIGV), F32),
            pltpu.VMEM((BLOCKS, 2 * BASIS, 2 * EIGV), BF16),
            pltpu.VMEM((2, BLOCKS, *block), BF16),
            pltpu.VMEM((2, CHUNKS, HALF, *block), BF16),
            pltpu.VMEM((2, CHUNKS, HALF, *block), BF16),
            pltpu.VMEM((2, CHUNKS, Y - 1, HALF, *block), BF16),
            pltpu.VMEM((2, BLOCKS, *block), BF16),
            pltpu.VMEM(spectral, BF16),
            pltpu.VMEM((X - 1, *spectral), BF16),
            pltpu.VMEM(spectral, BF16),
            pltpu.VMEM((Z - 1, *spectral), BF16),
            sem((2, BLOCKS // GROUP)),
            sem((2,)),
            sem((2, CHUNKS)),
            sem((2, CHUNKS)),
            sem((2, CHUNKS, Y - 1)),
            sem((2, CHUNKS, Y - 1)),
            sem((2, CHUNKS)),
            sem((2, CHUNKS)),
            sem((X - 1,)),
            sem((X - 1,)),
            sem((Z - 1,)),
            sem((Z - 1,)),
        ],
        compiler_params=pltpu.CompilerParams(
            collective_id=0, has_side_effects=True, vmem_limit_bytes=24 << 20
        ),
    )(*args)

    return pl.pallas_call(
        prolong,
        out_shape=jax.ShapeDtypeStruct((2, BLOCKS, COLS, COMP), F32),
        in_specs=[vmem_spec, vmem_spec],
        out_specs=hbm_spec,
        scratch_shapes=[pltpu.VMEM((2, BLOCKS, COLS, COMP), F32), sem((CHUNKS,))],
        compiler_params=pltpu.CompilerParams(vmem_limit_bytes=16 << 20),
    )(lift, bas)


def solution(mesh):
    in_specs = (
        P(None, "region", None, "eig"),
        P(None, "region", None, "eig"),
        P(None, "region", None, "eig"),
        P("eig"),
    )
    out_specs = P(None, "region", None, "eig")
    return jax.shard_map(shards, mesh=mesh, in_specs=in_specs, out_specs=out_specs, check_vma=False)
```

time: 50.1 us -> 39.6 us (0.79)
  local copies, waits for them, and re-layouts: 5.79 us -> 0 us
  Pallas kernels: 44.1 us -> 39.5 us
    unnamed x8 -> x0, local copies, waits for them, and re-layouts: 5.79 us -> none
    pallas_call x1, Pallas kernels: 40.8 us -> 37.7 us  [shards(): pl.pallas_call(coefficients, out_shape=(jax.ShapeDtypeStruct((BLOCKS, 2 *...]
    pallas_call x1, Pallas kernels: 3.33 us -> 1.75 us  [shards(): pl.pallas_call(prolong, out_shape=jax.ShapeDtypeStruct((2, BLOCKS, COLS,...]
where the time goes in v2:
time: 39.6 us; the launch traced here: 39.5 us
  Pallas kernels  39.5 us (100%)
    pallas_call x1, Pallas kernels, shards(): pl.pallas_call(coefficients, out_shape=(jax.ShapeDtypeStruct((BLOCKS, 2 *...  37.7 us
    pallas_call x1, Pallas kernels, shards(): pl.pallas_call(prolong, out_shape=jax.ShapeDtypeStruct((2, BLOCKS, COLS,...  1.75 us

profile of v2, /device:TPU:1, one launch (start us, length us, event | category | flops | bytes accessed | tf_op | source)
XLA Modules:
  0.0 39.5 jit_solution(2073434094484039692)
XLA Ops:
  0.0 37.7 %shard_map.46 = (bf16[24,128,384]{2,1,0:T(8,128)(2,1)S(1)}, bf16[24,32,128]{2,1,0:T(8,128)(2,1)S(1)}) custom-call(f32[2,24,32,384]{3,2,1,0:T(8,128)} %res.1, f32[2,24,64,384]{3,2,1,0:T(8,128)} %bas.1, bf16[2,24,64,128]{3,2,1,0:T(8,128)(2,1)} %eig.1, f32[1,128]{1,0:T(1,128)} %bitcast.1), custom_call_target="tpu_custom_call" | custom-call | tf_op jit(solution)/shard_map/pallas_call | solution.py:254
  37.7 1.8 %shard_map.47 = f32[2,24,32,384]{3,2,1,0:T(8,128)} custom-call(bf16[24,32,128]{2,1,0:T(8,128)(2,1)S(1)} %get-tuple-element.7.lift, bf16[24,128,384]{2,1,0:T(8,128)(2,1)S(1)} %get-tuple-element.8.bas), custom_call_target="tpu_custom_call" | custom-call | tf_op jit(solution)/shard_map/pallas_call | solution.py:295

commit v3 on v2

v3 whole, which is shorter than its diff:
```python
import functools

import jax
import jax.numpy as jnp
from jax import lax
from jax.experimental import pallas as pl
from jax.experimental.pallas import tpu as pltpu
from jax.sharding import PartitionSpec as P

MESH = pl.DeviceIdType.MESH
BF16 = jnp.bfloat16
F32 = jnp.float32

BLOCKS = 24
COLS = 32
BASIS = 64
COMP = 384
EIGV = 128
X, Y, Z = 4, 4, 8
CHUNK = 4
HALF = CHUNK // 2
CHUNKS = BLOCKS // CHUNK
LAG = 2
GROUP = 4
ALONG_X = (2, 1, 3)
ALONG_Y = (2, 1, 3)
ALONG_Z = (4, 3, 5, 2, 6, 1, 7)
ALONG_X_CORE = ((2, 0), (2, 1), (1, 0), (1, 1), (3, 0), (3, 1), (0, 1))


def signs(rows):
    lane = lax.broadcasted_iota(jnp.int32, (rows, 2 * BASIS), 1)
    return jnp.where(lane < BASIS, 1.0, -1.0).astype(F32)


def coefficients(
    res,
    bas,
    eig,
    wts,
    out,
    loaded,
    basis,
    ev,
    ev_in,
    wtv,
    wv,
    wv_in,
    part,
    core_in,
    chip,
    chip_in,
    whole,
    spec,
    spec_in,
    zown,
    zin,
    load_sem,
    eig_sem,
    e_send,
    e_recv,
    c_send,
    c_recv,
    y_send,
    y_recv,
    g_send,
    g_recv,
    x_send,
    x_recv,
    z_send,
    z_recv,
    met,
):
    region = lax.axis_index("region")
    me = lax.axis_index("eig")
    x, z = lax.rem(region, X), lax.div(region, X)
    core, y = lax.rem(me, 2), lax.div(me, 2)

    partner = (region, y * 2 + 1 - core)
    x_peers = [
        (z * X + lax.rem(x + d, X), y * 2 + lax.rem(core + dc, 2)) for d, dc in ALONG_X_CORE
    ]
    y_peers = [(region, lax.rem(y + d, Y) * 2 + core) for d in ALONG_Y]
    z_peers = [(lax.rem(z + d, Z) * X + x, me) for d in ALONG_Z]
    barrier = pltpu.get_barrier_semaphore()

    def greet(sem, peer):
        pl.semaphore_signal(sem, inc=1, device_id=peer, device_id_type=MESH)

    for d in ALONG_Z:
        greet(barrier, (lax.rem(z + d, Z) * X + x, y * 2 + 1))
    for d in ALONG_X:
        greet(barrier, (z * X + lax.rem(x + d, X), y * 2 + 1))
    for d in ALONG_Y:
        greet(barrier, (region, lax.rem(y + d, Y) * 2))
    greet(barrier, partner)

    loads = []
    for g in range(BLOCKS // GROUP):
        span = pl.ds(g * GROUP, GROUP)
        into = loaded.at[:, span]
        pltpu.make_async_copy(bas.at[:, span], into.at[:, :, COLS:], load_sem.at[g]).start()
        pltpu.make_async_copy(res.at[:, span], into.at[:, :, :COLS], load_sem.at[g]).start()
        loads.append(into)
    eig_load = pltpu.make_async_copy(eig, ev, eig_sem.at[0])
    wts_load = pltpu.make_async_copy(wts, wtv, eig_sem.at[1])
    eig_load.start()
    wts_load.start()

    def meet_chips(counter, others):
        @pl.when(core == counter)
        def _():
            pl.semaphore_wait(barrier, others)
            greet(met, partner)

        @pl.when(core != counter)
        def _():
            pl.semaphore_wait(met, 1)

    def arrived(ref, sem):
        pltpu.make_async_copy(ref, ref, sem).wait()

    def send(src, dst, send_sem, recv_sem, peer):
        pltpu.make_async_remote_copy(
            src_ref=src,
            dst_ref=dst,
            send_sem=send_sem,
            recv_sem=recv_sem,
            device_id=peer,
            device_id_type=MESH,
        ).start()

    def mine(c):
        return pl.ds(CHUNK * c + HALF * core, HALF)

    def to_partner(w, c):
        theirs = pl.ds(CHUNK * c + HALF * (1 - core), HALF)
        send(part.at[w, theirs], core_in.at[w, c], c_send, c_recv.at[w, c], partner)

    def along_y(w, c):
        arrived(core_in.at[w, c], c_recv.at[w, c])
        total = part[w, mine(c)].astype(F32) + core_in[w, c].astype(F32)
        chip[w, c] = total.astype(BF16)
        for i, peer in enumerate(y_peers):
            send(chip.at[w, c], chip_in.at[w, c, i], y_send, y_recv.at[w, c], peer)

    def over_y(w, c):
        arrived(chip_in.at[w, c], y_recv.at[w, c])
        total = chip[w, c].astype(F32)
        for i in range(len(y_peers)):
            total += chip_in[w, c, i].astype(F32)
        return total.astype(BF16)

    def blocks_of(c):
        return range(CHUNK * c, CHUNK * (c + 1))

    sign = signs(COLS)

    def project(c):
        for g in range(c * CHUNK // GROUP, (c + 1) * CHUNK // GROUP):
            arrived(loads[g], load_sem.at[g])
            for b in range(g * GROUP, (g + 1) * GROUP):
                r = jnp.concatenate([loaded[0, b, :COLS], loaded[1, b, :COLS]], 0).astype(BF16)
                k = jnp.concatenate([loaded[0, b, COLS:], loaded[1, b, COLS:]], 0).astype(BF16)
                basis[b] = k
                p = lax.dot_general(r, k, (((1,), (1,)), ((), ())), preferred_element_type=F32)
                part[0, b] = (p[:COLS] * sign + pltpu.roll(p[COLS:], BASIS, 1)).astype(BF16)

    def as_real(to, re, im):
        to[:BASIS, :EIGV] = re
        to[:BASIS, EIGV:] = -im
        to[BASIS:, :EIGV] = im
        to[BASIS:, EIGV:] = re

    def swap():
        eig_load.wait()
        for c in range(CHUNKS):
            theirs = pl.ds(CHUNK * c + HALF * (1 - core), HALF)
            send(ev.at[:, theirs], ev_in.at[:, c], e_send, e_recv, partner)

    for c in range(CHUNKS):
        project(c)
        if c == 0:
            meet_chips(0, 2 * (Y - 1) + 1)
        to_partner(0, c)
        if c >= LAG:
            along_y(0, c - LAG)
    swap()
    for c in range(CHUNKS - LAG, CHUNKS):
        along_y(0, c)
    for b in range(BLOCKS):
        as_real(wv.at[b], ev[0, b], ev[1, b])
    arrived(ev_in, e_recv)
    for c in range(CHUNKS):
        for i in range(HALF):
            as_real(wv_in.at[c, i], ev_in[0, c, i], ev_in[1, c, i])
    wts_load.wait()
    meet_chips(1, 2 * (X - 1) + 2 * (Z - 1) + 1)
    total = jnp.zeros((COLS, 2 * EIGV), F32)
    other = jnp.zeros((COLS, 2 * EIGV), F32)
    for c in range(CHUNKS):
        half = over_y(0, c)
        for i in range(HALF):
            total += jnp.dot(
                half[i], wv[CHUNK * c + HALF * core + i], preferred_element_type=F32
            )
            other += jnp.dot(half[i], wv_in[c, i], preferred_element_type=F32)

    spec[0] = total.astype(BF16)
    spec[1] = other.astype(BF16)
    for i, (d, peer) in enumerate(zip(ALONG_X_CORE, x_peers)):
        send(spec.at[d[1]], spec_in.at[i], x_send, x_recv, peer)
    arrived(spec_in, x_recv)
    for i in range(len(x_peers)):
        total += spec_in[i].astype(F32)
    zown[...] = total.astype(BF16)
    for i, peer in enumerate(z_peers):
        send(zown, zin.at[i], z_send, z_recv, peer)
    arrived(zin, z_recv)
    for i in range(len(z_peers)):
        total += zin[i].astype(F32)
    weighted = (total * jnp.concatenate([wtv[...], wtv[...]], 1)).astype(BF16)

    def expand(c):
        for b in blocks_of(c):
            part[1, b] = lax.dot_general(
                weighted, wv[b], (((1,), (1,)), ((), ())), preferred_element_type=F32
            ).astype(BF16)

    def prolong(c):
        for b in blocks_of(c):
            l = whole[b].astype(F32)
            rows = jnp.concatenate([l * sign, pltpu.roll(l, BASIS, 1)], 0).astype(BF16)
            both = jnp.dot(rows, basis[b], preferred_element_type=F32)
            out[0, b] = both[:COLS]
            out[1, b] = both[COLS:]

    for c in range(CHUNKS):
        expand(c)
        to_partner(1, c)
    for c in range(CHUNKS):
        along_y(1, c)
    for c in range(CHUNKS + 2):
        if c < CHUNKS:
            whole[mine(c)] = over_y(1, c)
            done = whole.at[mine(c)]
            send(done, done, g_send, g_recv.at[c], partner)
        if c >= 2:
            arrived(whole.at[pl.ds(CHUNK * (c - 2), HALF)], g_recv.at[c - 2])
            prolong(c - 2)
    arrived(ev_in, e_send)
    arrived(core_in, c_send)
    arrived(chip_in, y_send)
    arrived(spec_in, x_send)
    arrived(zin, z_send)
    arrived(whole.at[pl.ds(0, BLOCKS // 2)], g_send)


def write(ready, out, sem):
    copies = []
    for c in range(CHUNKS):
        span = pl.ds(CHUNK * c, CHUNK)
        copies.append(pltpu.make_async_copy(ready.at[:, span], out.at[:, span], sem.at[c]))
        copies[-1].start()
    for copy in copies:
        copy.wait()


def shards(residual, basis, eigvecs, weights):
    hbm_spec = pl.BlockSpec(memory_space=pltpu.HBM)
    vmem_spec = pl.BlockSpec(memory_space=pltpu.VMEM)
    sem = pltpu.SemaphoreType.DMA
    block = (COLS, 2 * BASIS)
    spectral = (COLS, 2 * EIGV)
    args = [
        pltpu.with_memory_space_constraint(a, pltpu.HBM)
        for a in (residual, basis, eigvecs, weights.reshape(1, EIGV))
    ]
    ready = pl.pallas_call(
        coefficients,
        out_shape=jax.ShapeDtypeStruct((2, BLOCKS, COLS, COMP), F32),
        in_specs=[hbm_spec] * 4,
        out_specs=vmem_spec,
        scratch_shapes=[
            pltpu.VMEM((2, BLOCKS, COLS + BASIS, COMP), F32),
            pltpu.VMEM((BLOCKS, 2 * BASIS, COMP), BF16),
            pltpu.VMEM((2, BLOCKS, BASIS, EIGV), BF16),
            pltpu.VMEM((2, CHUNKS, HALF, BASIS, EIGV), BF16),
            pltpu.VMEM((1, EIGV), F32),
            pltpu.VMEM((BLOCKS, 2 * BASIS, 2 * EIGV), BF16),
            pltpu.VMEM((CHUNKS, HALF, 2 * BASIS, 2 * EIGV), BF16),
            pltpu.VMEM((2, BLOCKS, *block), BF16),
            pltpu.VMEM((2, CHUNKS, HALF, *block), BF16),
            pltpu.VMEM((2, CHUNKS, HALF, *block), BF16),
            pltpu.VMEM((2, CHUNKS, Y - 1, HALF, *block), BF16),
            pltpu.VMEM((BLOCKS, *block), BF16),
            pltpu.VMEM((2, *spectral), BF16),
            pltpu.VMEM((2 * X - 1, *spectral), BF16),
            pltpu.VMEM(spectral, BF16),
            pltpu.VMEM((Z - 1, *spectral), BF16),
            sem((BLOCKS // GROUP,)),
            sem((2,)),
            sem,
            sem,
            sem,
            sem((2, CHUNKS)),
            sem,
            sem((2, CHUNKS)),
            sem,
            sem((CHUNKS,)),
            sem,
            sem,
            sem,
            sem,
            pltpu.SemaphoreType.REGULAR,
        ],
        compiler_params=pltpu.CompilerParams(
            collective_id=0, has_side_effects=True, vmem_limit_bytes=24 << 20
        ),
    )(*args)

    return pl.pallas_call(
        write,
        out_shape=jax.ShapeDtypeStruct((2, BLOCKS, COLS, COMP), F32),
        in_specs=[vmem_spec],
        out_specs=hbm_spec,
        scratch_shapes=[sem((CHUNKS,))],
        compiler_params=pltpu.CompilerParams(vmem_limit_bytes=16 << 20),
    )(ready)


def solution(mesh):
    in_specs = (
        P(None, "region", None, "eig"),
        P(None, "region", None, "eig"),
        P(None, "region", None, "eig"),
        P("eig"),
    )
    out_specs = P(None, "region", None, "eig")
    return jax.shard_map(shards, mesh=mesh, in_specs=in_specs, out_specs=out_specs, check_vma=False)
```

time: 39.6 us -> 38.3 us (0.967)
  Pallas kernels: 39.5 us -> 38.2 us
    pallas_call x2, Pallas kernels: 39.5 us -> 38.2 us  [the longest x1 36.8 us: shards(): pl.pallas_call(coefficients, out_shape=jax.ShapeDtypeStruct((2, BLOCKS, C...]
where the time goes in v3:
time: 38.3 us; the launch traced here: 38.2 us
  Pallas kernels  38.2 us (100%)
    pallas_call x1, Pallas kernels, shards(): pl.pallas_call(coefficients, out_shape=jax.ShapeDtypeStruct((2, BLOCKS, C...  36.8 us
    pallas_call x1, Pallas kernels, shards(): pl.pallas_call(write, out_shape=jax.ShapeDtypeStruct((2, BLOCKS, COLS, CO...  1.45 us

profile of v3, /device:TPU:1, one launch (start us, length us, event | category | flops | bytes accessed | tf_op | source)
XLA Modules:
  0.0 38.2 jit_solution(3837874905216078481)
XLA Ops:
  0.0 36.8 %shard_map.46.ready = f32[2,24,32,384]{3,2,1,0:T(8,128)S(1)} custom-call(f32[2,24,32,384]{3,2,1,0:T(8,128)} %res.1, f32[2,24,64,384]{3,2,1,0:T(8,128)} %bas.1, bf16[2,24,64,128]{3,2,1,0:T(8,128)(2,1)} %eig.1, f32[1,128]{1,0:T(1,128)} %bitcast.1), custom_call_target="tpu_custom_call" | custom-call | tf_op jit(solution)/shard_map/pallas_call | solution.py:279
  36.8 1.4 %shard_map.47 = f32[2,24,32,384]{3,2,1,0:T(8,128)} custom-call(f32[2,24,32,384]{3,2,1,0:T(8,128)S(1)} %shard_map.46.ready), custom_call_target="tpu_custom_call" | custom-call | tf_op jit(solution)/shard_map/pallas_call | solution.py:322

commit v4 on v3

--- a/solution.py
+++ b/solution.py
@@ -20,11 +20,12 @@
 CHUNK = 4
 HALF = CHUNK // 2
 CHUNKS = BLOCKS // CHUNK
-LAG = 2
+BEFORE = 3
 GROUP = 4
 ALONG_X = (2, 1, 3)
 ALONG_Y = (2, 1, 3)
 ALONG_Z = (4, 3, 5, 2, 6, 1, 7)
+ALONG_Y_CORE = ((2, 0), (2, 1), (1, 0), (1, 1), (3, 0), (3, 1))
 ALONG_X_CORE = ((2, 0), (2, 1), (1, 0), (1, 1), (3, 0), (3, 1), (0, 1))
 
 
@@ -50,6 +51,8 @@
     core_in,
     chip,
     chip_in,
+    first_in,
+    last_in,
     whole,
     spec,
     spec_in,
@@ -63,6 +66,10 @@
     c_recv,
     y_send,
     y_recv,
+    f_send,
+    f_recv,
+    l_send,
+    l_recv,
     g_send,
     g_recv,
     x_send,
@@ -80,6 +87,9 @@
     x_peers = [
         (z * X + lax.rem(x + d, X), y * 2 + lax.rem(core + dc, 2)) for d, dc in ALONG_X_CORE
     ]
+    y_both = [
+        (region, lax.rem(y + d, Y) * 2 + lax.rem(core + dc, 2)) for d, dc in ALONG_Y_CORE
+    ]
     y_peers = [(region, lax.rem(y + d, Y) * 2 + core) for d in ALONG_Y]
     z_peers = [(lax.rem(z + d, Z) * X + x, me) for d in ALONG_Z]
     barrier = pltpu.get_barrier_semaphore()
@@ -137,18 +147,40 @@
         theirs = pl.ds(CHUNK * c + HALF * (1 - core), HALF)
         send(part.at[w, theirs], core_in.at[w, c], c_send, c_recv.at[w, c], partner)
 
+    def straight(w):
+        to_partner(w, 0)
+        for i, ((_, dc), peer) in enumerate(zip(ALONG_Y_CORE, y_both)):
+            half = pl.ds(HALF * lax.rem(core + dc, 2), HALF)
+            send(part.at[w, half], first_in.at[w, i], f_send, f_recv.at[w], peer)
+
+    def slot(w, c):
+        return w * (CHUNKS - 1) + c - 1
+
     def along_y(w, c):
         arrived(core_in.at[w, c], c_recv.at[w, c])
         total = part[w, mine(c)].astype(F32) + core_in[w, c].astype(F32)
         chip[w, c] = total.astype(BF16)
-        for i, peer in enumerate(y_peers):
-            send(chip.at[w, c], chip_in.at[w, c, i], y_send, y_recv.at[w, c], peer)
+        if w == 1 and c == CHUNKS - 1:
+            for i, peer in enumerate(y_both + [partner]):
+                send(chip.at[w, c], last_in.at[i], l_send, l_recv, peer)
+        else:
+            k = slot(w, c)
+            for i, peer in enumerate(y_peers):
+                send(chip.at[w, c], chip_in.at[k, i], y_send, y_recv.at[k], peer)
 
     def over_y(w, c):
-        arrived(chip_in.at[w, c], y_recv.at[w, c])
-        total = chip[w, c].astype(F32)
-        for i in range(len(y_peers)):
-            total += chip_in[w, c, i].astype(F32)
+        if c == 0:
+            arrived(core_in.at[w, c], c_recv.at[w, c])
+            arrived(first_in.at[w], f_recv.at[w])
+            total = part[w, mine(c)].astype(F32) + core_in[w, c].astype(F32)
+            for i in range(len(y_both)):
+                total += first_in[w, i].astype(F32)
+        else:
+            k = slot(w, c)
+            arrived(chip_in.at[k], y_recv.at[k])
+            total = chip[w, c].astype(F32)
+            for i in range(len(y_peers)):
+                total += chip_in[k, i].astype(F32)
         return total.astype(BF16)
 
     def blocks_of(c):
@@ -178,16 +210,20 @@
             theirs = pl.ds(CHUNK * c + HALF * (1 - core), HALF)
             send(ev.at[:, theirs], ev_in.at[:, c], e_send, e_recv, partner)
 
-    for c in range(CHUNKS):
+    for c in range(BEFORE):
         project(c)
-        if c == 0:
-            meet_chips(0, 2 * (Y - 1) + 1)
+    meet_chips(0, 2 * (Y - 1) + 1)
+    straight(0)
+    for c in range(1, BEFORE):
         to_partner(0, c)
-        if c >= LAG:
-            along_y(0, c - LAG)
+    for c in range(BEFORE, CHUNKS):
+        project(c)
+        to_partner(0, c)
+        if c > BEFORE:
+            along_y(0, c - BEFORE)
+    for c in range(CHUNKS - BEFORE, CHUNKS):
+        along_y(0, c)
     swap()
-    for c in range(CHUNKS - LAG, CHUNKS):
-        along_y(0, c)
     for b in range(BLOCKS):
         as_real(wv.at[b], ev[0, b], ev[1, b])
     arrived(ev_in, e_recv)
@@ -235,25 +271,41 @@
             out[0, b] = both[:COLS]
             out[1, b] = both[COLS:]
 
-    for c in range(CHUNKS):
+    expand(0)
+    straight(1)
+    for c in range(1, CHUNKS):
         expand(c)
         to_partner(1, c)
-    for c in range(CHUNKS):
+    for c in range(1, CHUNKS):
         along_y(1, c)
-    for c in range(CHUNKS + 2):
-        if c < CHUNKS:
+    last = CHUNKS - 1
+    for c in range(last + 2):
+        if c < last:
             whole[mine(c)] = over_y(1, c)
             done = whole.at[mine(c)]
             send(done, done, g_send, g_recv.at[c], partner)
         if c >= 2:
             arrived(whole.at[pl.ds(CHUNK * (c - 2), HALF)], g_recv.at[c - 2])
             prolong(c - 2)
+    arrived(last_in, l_recv)
+    ours = chip[1, last].astype(F32)
+    theirs = last_in[len(y_both)].astype(F32)
+    for i, (_, dc) in enumerate(ALONG_Y_CORE):
+        if dc == 0:
+            ours += last_in[i].astype(F32)
+        else:
+            theirs += last_in[i].astype(F32)
+    whole[mine(last)] = ours.astype(BF16)
+    whole[pl.ds(CHUNK * last + HALF * (1 - core), HALF)] = theirs.astype(BF16)
+    prolong(last)
     arrived(ev_in, e_send)
     arrived(core_in, c_send)
     arrived(chip_in, y_send)
+    arrived(first_in, f_send)
+    arrived(last_in, l_send)
     arrived(spec_in, x_send)
     arrived(zin, z_send)
-    arrived(whole.at[pl.ds(0, BLOCKS // 2)], g_send)
+    arrived(whole.at[pl.ds(0, HALF * (CHUNKS - 1))], g_send)
 
 
 def write(ready, out, sem):
@@ -292,7 +344,9 @@
             pltpu.VMEM((2, BLOCKS, *block), BF16),
             pltpu.VMEM((2, CHUNKS, HALF, *block), BF16),
             pltpu.VMEM((2, CHUNKS, HALF, *block), BF16),
-            pltpu.VMEM((2, CHUNKS, Y - 1, HALF, *block), BF16),
+            pltpu.VMEM((2 * CHUNKS - 3, Y - 1, HALF, *block), BF16),
+            pltpu.VMEM((2, 2 * Y - 2, HALF, *block), BF16),
+            pltpu.VMEM((2 * Y - 1, HALF, *block), BF16),
             pltpu.VMEM((BLOCKS, *block), BF16),
             pltpu.VMEM((2, *spectral), BF16),
             pltpu.VMEM((2 * X - 1, *spectral), BF16),
@@ -305,9 +359,13 @@
             sem,
             sem((2, CHUNKS)),
             sem,
-            sem((2, CHUNKS)),
-            sem,
-            sem((CHUNKS,)),
+            sem((2 * CHUNKS - 3,)),
+            sem,
+            sem((2,)),
+            sem,
+            sem,
+            sem,
+            sem((CHUNKS - 1,)),
             sem,
             sem,
             sem,

time: 38.3 us -> 37.8 us (0.987)
  Pallas kernels: 38.2 us -> 37.8 us
    pallas_call x1, Pallas kernels: 36.8 us -> 36.3 us  [shards(): pl.pallas_call(coefficients, out_shape=jax.ShapeDtypeStruct((2, BLOCKS, C...]
where the time goes in v4:
time: 37.8 us
  Pallas kernels  37.8 us (100%)
    pallas_call x1, Pallas kernels, shards(): pl.pallas_call(coefficients, out_shape=jax.ShapeDtypeStruct((2, BLOCKS, C...  36.3 us
    pallas_call x1, Pallas kernels, shards(): pl.pallas_call(write, out_shape=jax.ShapeDtypeStruct((2, BLOCKS, COLS, CO...  1.45 us

profile of v4, /device:TPU:1, one launch (start us, length us, event | category | flops | bytes accessed | tf_op | source)
XLA Modules:
  0.0 37.8 jit_solution(10274583850580285033)
XLA Ops:
  0.0 36.3 %shard_map.46.ready = f32[2,24,32,384]{3,2,1,0:T(8,128)S(1)} custom-call(f32[2,24,32,384]{3,2,1,0:T(8,128)} %res.1, f32[2,24,64,384]{3,2,1,0:T(8,128)} %bas.1, bf16[2,24,64,128]{3,2,1,0:T(8,128)(2,1)} %eig.1, f32[1,128]{1,0:T(1,128)} %bitcast.1), custom_call_target="tpu_custom_call" | custom-call | tf_op jit(solution)/shard_map/pallas_call | solution.py:331
  36.3 1.4 %shard_map.47 = f32[2,24,32,384]{3,2,1,0:T(8,128)} custom-call(f32[2,24,32,384]{3,2,1,0:T(8,128)S(1)} %shard_map.46.ready), custom_call_target="tpu_custom_call" | custom-call | tf_op jit(solution)/shard_map/pallas_call | solution.py:380

commit v5 on v4

--- a/solution.py
+++ b/solution.py
@@ -20,6 +20,7 @@
 CHUNK = 4
 HALF = CHUNK // 2
 CHUNKS = BLOCKS // CHUNK
+EARLY = 4
 BEFORE = 3
 GROUP = 4
 ALONG_X = (2, 1, 3)
@@ -34,14 +35,21 @@
     return jnp.where(lane < BASIS, 1.0, -1.0).astype(F32)
 
 
+def prolong(lift, bas, sign):
+    l = lift.astype(F32)
+    rows = jnp.concatenate([l * sign, pltpu.roll(l, BASIS, 1)], 0).astype(BF16)
+    return jnp.dot(rows, bas, preferred_element_type=F32)
+
+
 def coefficients(
     res,
     bas,
     eig,
     wts,
     out,
+    lift_out,
+    basis,
     loaded,
-    basis,
     ev,
     ev_in,
     wtv,
@@ -97,10 +105,6 @@
     def greet(sem, peer):
         pl.semaphore_signal(sem, inc=1, device_id=peer, device_id_type=MESH)
 
-    for d in ALONG_Z:
-        greet(barrier, (lax.rem(z + d, Z) * X + x, y * 2 + 1))
-    for d in ALONG_X:
-        greet(barrier, (z * X + lax.rem(x + d, X), y * 2 + 1))
     for d in ALONG_Y:
         greet(barrier, (region, lax.rem(y + d, Y) * 2))
     greet(barrier, partner)
@@ -117,6 +121,10 @@
     eig_load.start()
     wts_load.start()
 
+    for d in ALONG_Z:
+        greet(barrier, (lax.rem(z + d, Z) * X + x, y * 2 + 1))
+    for d in ALONG_X:
+        greet(barrier, (z * X + lax.rem(x + d, X), y * 2 + 1))
     def meet_chips(counter, others):
         @pl.when(core == counter)
         def _():
@@ -263,14 +271,6 @@
                 weighted, wv[b], (((1,), (1,)), ((), ())), preferred_element_type=F32
             ).astype(BF16)
 
-    def prolong(c):
-        for b in blocks_of(c):
-            l = whole[b].astype(F32)
-            rows = jnp.concatenate([l * sign, pltpu.roll(l, BASIS, 1)], 0).astype(BF16)
-            both = jnp.dot(rows, basis[b], preferred_element_type=F32)
-            out[0, b] = both[:COLS]
-            out[1, b] = both[COLS:]
-
     expand(0)
     straight(1)
     for c in range(1, CHUNKS):
@@ -286,7 +286,13 @@
             send(done, done, g_send, g_recv.at[c], partner)
         if c >= 2:
             arrived(whole.at[pl.ds(CHUNK * (c - 2), HALF)], g_recv.at[c - 2])
-            prolong(c - 2)
+            for b in blocks_of(c - 2):
+                if c - 2 < EARLY:
+                    both = prolong(whole[b], basis[b], sign)
+                    out[0, b] = both[:COLS]
+                    out[1, b] = both[COLS:]
+                else:
+                    lift_out[b - CHUNK * EARLY] = whole[b]
     arrived(last_in, l_recv)
     ours = chip[1, last].astype(F32)
     theirs = last_in[len(y_both)].astype(F32)
@@ -295,9 +301,9 @@
             ours += last_in[i].astype(F32)
         else:
             theirs += last_in[i].astype(F32)
-    whole[mine(last)] = ours.astype(BF16)
-    whole[pl.ds(CHUNK * last + HALF * (1 - core), HALF)] = theirs.astype(BF16)
-    prolong(last)
+    first = CHUNK * (last - EARLY)
+    lift_out[pl.ds(first + HALF * core, HALF)] = ours.astype(BF16)
+    lift_out[pl.ds(first + HALF * (1 - core), HALF)] = theirs.astype(BF16)
     arrived(ev_in, e_send)
     arrived(core_in, c_send)
     arrived(chip_in, y_send)
@@ -308,12 +314,23 @@
     arrived(whole.at[pl.ds(0, HALF * (CHUNKS - 1))], g_send)
 
 
-def write(ready, out, sem):
+def write(ready, lift, basis, out, rest, sem):
+    sign = signs(COLS)
     copies = []
-    for c in range(CHUNKS):
+
+    def start(c, source):
         span = pl.ds(CHUNK * c, CHUNK)
-        copies.append(pltpu.make_async_copy(ready.at[:, span], out.at[:, span], sem.at[c]))
+        copies.append(pltpu.make_async_copy(source, out.at[:, span], sem.at[c]))
         copies[-1].start()
+
+    for c in range(EARLY):
+        start(c, ready.at[:, pl.ds(CHUNK * c, CHUNK)])
+    for c in range(EARLY, CHUNKS):
+        for b in range(CHUNK * (c - EARLY), CHUNK * (c - EARLY + 1)):
+            both = prolong(lift[b], basis[CHUNK * EARLY + b], sign)
+            rest[0, b] = both[:COLS]
+            rest[1, b] = both[COLS:]
+        start(c, rest.at[:, pl.ds(CHUNK * (c - EARLY), CHUNK)])
     for copy in copies:
         copy.wait()
 
@@ -328,14 +345,18 @@
         pltpu.with_memory_space_constraint(a, pltpu.HBM)
         for a in (residual, basis, eigvecs, weights.reshape(1, EIGV))
     ]
-    ready = pl.pallas_call(
+    early = CHUNK * EARLY
+    done = pl.pallas_call(
         coefficients,
-        out_shape=jax.ShapeDtypeStruct((2, BLOCKS, COLS, COMP), F32),
+        out_shape=(
+            jax.ShapeDtypeStruct((2, early, COLS, COMP), F32),
+            jax.ShapeDtypeStruct((BLOCKS - early, *block), BF16),
+            jax.ShapeDtypeStruct((BLOCKS, 2 * BASIS, COMP), BF16),
+        ),
         in_specs=[hbm_spec] * 4,
-        out_specs=vmem_spec,
+        out_specs=(vmem_spec, vmem_spec, vmem_spec),
         scratch_shapes=[
             pltpu.VMEM((2, BLOCKS, COLS + BASIS, COMP), F32),
-            pltpu.VMEM((BLOCKS, 2 * BASIS, COMP), BF16),
             pltpu.VMEM((2, BLOCKS, BASIS, EIGV), BF16),
             pltpu.VMEM((2, CHUNKS, HALF, BASIS, EIGV), BF16),
             pltpu.VMEM((1, EIGV), F32),
@@ -380,11 +401,14 @@
     return pl.pallas_call(
         write,
         out_shape=jax.ShapeDtypeStruct((2, BLOCKS, COLS, COMP), F32),
-        in_specs=[vmem_spec],
+        in_specs=[vmem_spec] * 3,
         out_specs=hbm_spec,
-        scratch_shapes=[sem((CHUNKS,))],
+        scratch_shapes=[
+            pltpu.VMEM((2, BLOCKS - early, COLS, COMP), F32),
+            sem((CHUNKS,)),
+        ],
         compiler_params=pltpu.CompilerParams(vmem_limit_bytes=16 << 20),
-    )(ready)
+    )(*done)
 
 
 def solution(mesh):

time: 37.8 us -> 37.3 us (0.987)
  Pallas kernels: 37.8 us -> 37.2 us
    pallas_call x1, Pallas kernels: 36.3 us -> 35.8 us  [shards(): pl.pallas_call(coefficients, out_shape=(jax.ShapeDtypeStruct((2, early, C...]
where the time goes in v5:
time: 37.3 us
  Pallas kernels  37.2 us (100%)
    pallas_call x1, Pallas kernels, shards(): pl.pallas_call(coefficients, out_shape=(jax.ShapeDtypeStruct((2, early, C...  35.8 us
    pallas_call x1, Pallas kernels, shards(): pl.pallas_call(write, out_shape=jax.ShapeDtypeStruct((2, BLOCKS, COLS, CO...  1.47 us

profile of v5, /device:TPU:1, one launch (start us, length us, event | category | flops | bytes accessed | tf_op | source)
XLA Modules:
  0.0 37.3 jit_solution(13033927128805460561)
XLA Ops:
  0.0 35.8 %shard_map.46 = (f32[2,16,32,384]{3,2,1,0:T(8,128)S(1)}, bf16[8,32,128]{2,1,0:T(8,128)(2,1)S(1)}, bf16[24,128,384]{2,1,0:T(8,128)(2,1)S(1)}) custom-call(f32[2,24,32,384]{3,2,1,0:T(8,128)} %res.1, f32[2,24,64,384]{3,2,1,0:T(8,128)} %bas.1, bf16[2,24,64,128]{3,2,1,0:T(8,128)(2,1)} %eig.1, f32[1,128]{1,0:T(1,128)} %bitcast.1), custom_call_target="tpu_custom_call" | custom-call | tf_op jit(solution)/shard_map/pallas_call | solution.py:349
  35.8 1.5 %shard_map.47 = f32[2,24,32,384]{3,2,1,0:T(8,128)} custom-call(f32[2,16,32,384]{3,2,1,0:T(8,128)S(1)} %get-tuple-element.8.ready, bf16[8,32,128]{2,1,0:T(8,128)(2,1)S(1)} %get-tuple-element.9.lift, bf16[24,128,384]{2,1,0:T(8,128)(2,1)S(1)} %get-tuple-element.10.basis), custom_call_target="tpu_custom_call" | custom-call | tf_op jit(solution)/shard_map/pallas_call | solution.py:401

commit v6 on v5

--- a/solution.py
+++ b/solution.py
@@ -21,6 +21,7 @@
 HALF = CHUNK // 2
 CHUNKS = BLOCKS // CHUNK
 EARLY = 4
+JOINED = (3, 2)
 BEFORE = 3
 GROUP = 4
 ALONG_X = (2, 1, 3)
@@ -153,7 +154,7 @@
 
     def to_partner(w, c):
         theirs = pl.ds(CHUNK * c + HALF * (1 - core), HALF)
-        send(part.at[w, theirs], core_in.at[w, c], c_send, c_recv.at[w, c], partner)
+        send(part.at[w, theirs], core_in.at[w, c], c_send, c_recv.at[w, max(c - JOINED[w] + 1, 0)], partner)
 
     def straight(w):
         to_partner(w, 0)
@@ -165,7 +166,10 @@
         return w * (CHUNKS - 1) + c - 1
 
     def along_y(w, c):
-        arrived(core_in.at[w, c], c_recv.at[w, c])
+        if c == 1:
+            arrived(core_in.at[w, pl.ds(0, JOINED[w])], c_recv.at[w, 0])
+        elif c >= JOINED[w]:
+            arrived(core_in.at[w, c], c_recv.at[w, c - JOINED[w] + 1])
         total = part[w, mine(c)].astype(F32) + core_in[w, c].astype(F32)
         chip[w, c] = total.astype(BF16)
         if w == 1 and c == CHUNKS - 1:
@@ -178,7 +182,6 @@
 
     def over_y(w, c):
         if c == 0:
-            arrived(core_in.at[w, c], c_recv.at[w, c])
             arrived(first_in.at[w], f_recv.at[w])
             total = part[w, mine(c)].astype(F32) + core_in[w, c].astype(F32)
             for i in range(len(y_both)):
@@ -378,7 +381,7 @@
             sem,
             sem,
             sem,
-            sem((2, CHUNKS)),
+            sem((2, CHUNKS - min(JOINED) + 1)),
             sem,
             sem((2 * CHUNKS - 3,)),
             sem,

time: 37.3 us -> 37.3 us (level)
  no operation moved by 1% of the time
where the time goes in v6:
time: 37.3 us; the launch traced here: 37.2 us
  Pallas kernels  37.2 us (100%)
    pallas_call x1, Pallas kernels, shards(): pl.pallas_call(coefficients, out_shape=(jax.ShapeDtypeStruct((2, early, C...  35.8 us
    pallas_call x1, Pallas kernels, shards(): pl.pallas_call(write, out_shape=jax.ShapeDtypeStruct((2, BLOCKS, COLS, CO...  1.47 us

profile of v6, /device:TPU:1, one launch (start us, length us, event | category | flops | bytes accessed | tf_op | source)
XLA Modules:
  0.0 37.2 jit_solution(12306976515385817479)
XLA Ops:
  0.0 35.8 %shard_map.46 = (f32[2,16,32,384]{3,2,1,0:T(8,128)S(1)}, bf16[8,32,128]{2,1,0:T(8,128)(2,1)S(1)}, bf16[24,128,384]{2,1,0:T(8,128)(2,1)S(1)}) custom-call(f32[2,24,32,384]{3,2,1,0:T(8,128)} %res.1, f32[2,24,64,384]{3,2,1,0:T(8,128)} %bas.1, bf16[2,24,64,128]{3,2,1,0:T(8,128)(2,1)} %eig.1, f32[1,128]{1,0:T(1,128)} %bitcast.1), custom_call_target="tpu_custom_call" | custom-call | tf_op jit(solution)/shard_map/pallas_call | solution.py:352
  35.8 1.5 %shard_map.47 = f32[2,24,32,384]{3,2,1,0:T(8,128)} custom-call(f32[2,16,32,384]{3,2,1,0:T(8,128)S(1)} %get-tuple-element.8.ready, bf16[8,32,128]{2,1,0:T(8,128)(2,1)S(1)} %get-tuple-element.9.lift, bf16[24,128,384]{2,1,0:T(8,128)(2,1)S(1)} %get-tuple-element.10.basis), custom_call_target="tpu_custom_call" | custom-call | tf_op jit(solution)/shard_map/pallas_call | solution.py:404
